TPU v7x, 512 devices: a whole 4x8x8 slice. The times are simulated.
512 devices in a mesh: doc: 32 (over y, x), seq: 16 (over z, core).
Axes of the slice: x: 4, y: 8, z: 8, core: 2. Of those that a mesh axis runs over, the one named last changes fastest.
Arguments:
- tokens: bfloat16 [131072, 1024], P(('doc', 'seq')), parts along dimension 0, may hold values from -8 to 8
- bottom_qkv: bfloat16 [1024, 3072], P('seq'), may hold values from -1 to 1
- bottom_out: bfloat16 [1024, 1024], P('seq'), may hold values from -0.5 to 0.5
- top_qkv: bfloat16 [1024, 3, 1024], P(None, None, 'seq'), may hold values from -1 to 1
- top_out: bfloat16 [1024, 1024], P('seq'), may hold values from -0.5 to 0.5
- cross_query: bfloat16 [1024, 1024], P('seq'), may hold values from -1 to 1
- cross_kv: bfloat16 [1024, 2, 1024], P(None, None, 'seq'), may hold values from -1 to 1
- cross_out: bfloat16 [1024, 1024], P('seq'), may hold values from -0.5 to 0.5
Outputs:
- encoded: bfloat16 [131072, 1024], P(('doc', 'seq')), parts along dimension 0
There are 32 independent parts, one for each index of `doc`. A program takes and returns all parts, laid end to end along the dimension named above; an argument that names none is the same for every part. Nothing has to cross between parts.
All inputs are finite; a program needn't handle non-finite values.
Results may differ from a plain program's by a relative error of at most 0.013.
Values may be sent and summed in bfloat16 or wider, within the bound.
A program may use at most 64 MiB of HBM per device.

v0:
```python
import math
import jax
import jax.numpy as jnp
from jax import lax
from jax.sharding import PartitionSpec as P

H = 16
W = 512
POOL = 32
EPS = 1e-06


def padded(cells, sides, width):
    for axis, dim in sides:
        count = lax.axis_size(axis)
        ends = count - 1
        head = lax.slice_in_dim(cells, 0, width, axis=dim)
        tail = lax.slice_in_dim(cells, cells.shape[dim] - width, cells.shape[dim], axis=dim)
        cells = jnp.concatenate(
            [
                lax.ppermute(tail, axis, [(i, (i + 1) % count) for i in range(ends)]),
                cells,
                lax.ppermute(head, axis, [((i + 1) % count, i) for i in range(ends)]),
            ],
            axis=dim,
        )
    return cells


def normed(values_in):
    values_in = values_in.astype(jnp.float32)
    return (
        values_in * lax.rsqrt(jnp.mean(values_in * values_in, axis=-1, keepdims=True) + EPS)
    ).astype(jnp.bfloat16)


def window_mask(first_tok, tok_count, half_win, total_tok):
    query_pos = first_tok + jnp.arange(tok_count, dtype=jnp.int32)
    key_pos = first_tok - half_win + jnp.arange(tok_count + 2 * half_win, dtype=jnp.int32)
    offsets = key_pos[None, :] - query_pos[:, None]
    inside = (key_pos[None, :] >= 0) & (key_pos[None, :] < total_tok)
    return (offsets >= -half_win) & (offsets < half_win) & inside


def attend(queries, key_mat, value_mat, allowed, head_count):
    row_count = queries.shape[0]
    key_count = key_mat.shape[0]
    head_width = queries.shape[1] // head_count
    score_scale = 1.0 / math.sqrt(head_width)
    split_q = queries.reshape(row_count, head_count, head_width).transpose(1, 0, 2)
    split_k = key_mat.reshape(key_count, head_count, head_width).transpose(1, 0, 2)
    split_v = value_mat.reshape(key_count, head_count, head_width).transpose(1, 0, 2)

    def one_head(operands):
        query_h, key_h, value_h = operands
        scores = jnp.dot(query_h, key_h.T, preferred_element_type=jnp.float32) * score_scale
        if allowed is not None:
            scores = jnp.where(allowed, scores, -1e30)
        row_peak = jnp.max(scores, axis=1, keepdims=True)
        expo = jnp.exp(scores - row_peak)
        row_total = jnp.sum(expo, axis=1, keepdims=True)
        mixture = (
            jnp.dot(expo.astype(jnp.bfloat16), value_h, preferred_element_type=jnp.float32)
            / row_total
        )
        return mixture.astype(jnp.bfloat16)

    merged = lax.map(one_head, (split_q, split_k, split_v))
    return merged.transpose(1, 0, 2).reshape(row_count, head_count * head_width)


def fold_rows(operand, shard_rows):
    return jnp.dot(operand, shard_rows, preferred_element_type=jnp.float32)


def local(tokens, bottom_qkv, bottom_out, top_qkv, top_out, cross_query, cross_kv, cross_out):
    tok_count, model_width = tokens.shape
    devices_seq = lax.axis_size("seq")
    local_heads = H // devices_seq
    half_win = W // 2
    total_tok = tok_count * devices_seq
    first_tok = lax.axis_index("seq") * tok_count
    normed_tok = normed(tokens)
    project = fold_rows(normed_tok, lax.all_gather(bottom_qkv, "seq", axis=0, tiled=True))
    project = project.astype(jnp.bfloat16)
    queries = project[:, :model_width]
    key_vals = padded(project[:, model_width:], (("seq", 0),), half_win)
    allowed = window_mask(first_tok, tok_count, half_win, total_tok)
    attended = attend(queries, key_vals[:, :model_width], key_vals[:, model_width:], allowed, H)
    out_sum = fold_rows(attended, lax.all_gather(bottom_out, "seq", axis=0, tiled=True))
    lower_tok = (tokens.astype(jnp.float32) + out_sum).astype(jnp.bfloat16)
    pooled = jnp.mean(
        lower_tok.astype(jnp.float32).reshape(tok_count // POOL, POOL, model_width), axis=1
    ).astype(jnp.bfloat16)
    all_units = lax.all_gather(pooled, "seq", axis=0, tiled=True)
    unit_norm = normed(all_units)
    top_q = jnp.dot(unit_norm, top_qkv[:, 0, :], preferred_element_type=jnp.float32).astype(
        jnp.bfloat16
    )
    top_k = jnp.dot(unit_norm, top_qkv[:, 1, :], preferred_element_type=jnp.float32).astype(
        jnp.bfloat16
    )
    top_v = jnp.dot(unit_norm, top_qkv[:, 2, :], preferred_element_type=jnp.float32).astype(
        jnp.bfloat16
    )
    top_att = attend(top_q, top_k, top_v, None, local_heads)
    head_term = jnp.dot(top_att, top_out, preferred_element_type=jnp.float32)
    head_total = lax.psum(head_term.astype(jnp.bfloat16), "seq").astype(jnp.float32)
    top_units = (all_units.astype(jnp.float32) + head_total).astype(jnp.bfloat16)
    upper_norm = normed(top_units)
    part_keys = jnp.dot(upper_norm, cross_kv[:, 0, :], preferred_element_type=jnp.float32).astype(
        jnp.bfloat16
    )
    part_vals = jnp.dot(upper_norm, cross_kv[:, 1, :], preferred_element_type=jnp.float32).astype(
        jnp.bfloat16
    )
    stacked = jnp.concatenate([part_keys, part_vals], axis=1)
    gathered = lax.all_gather(stacked, "seq", axis=1, tiled=True)
    unit_count = gathered.shape[0]
    arranged = gathered.reshape(unit_count, devices_seq, 2, part_keys.shape[1])
    cross_keys = arranged[:, :, 0, :].reshape(unit_count, model_width)
    cross_vals = arranged[:, :, 1, :].reshape(unit_count, model_width)
    lower_norm = normed(lower_tok)
    query_acc = fold_rows(lower_norm, lax.all_gather(cross_query, "seq", axis=0, tiled=True))
    cross_q = query_acc.astype(jnp.bfloat16)
    cross_att = attend(cross_q, cross_keys, cross_vals, None, H)
    cross_sum = fold_rows(cross_att, lax.all_gather(cross_out, "seq", axis=0, tiled=True))
    return (lower_tok.astype(jnp.float32) + cross_sum).astype(jnp.bfloat16)


def solution(mesh):
    in_specs = (
        P(("doc", "seq"), None),
        P("seq", None),
        P("seq", None),
        P(None, None, "seq"),
        P("seq", None),
        P("seq", None),
        P(None, None, "seq"),
        P("seq", None),
    )
    out_specs = P(("doc", "seq"), None)
    return jax.shard_map(local, mesh=mesh, in_specs=in_specs, out_specs=out_specs, check_vma=False)
```

profile of v0, /device:TPU:1, one launch (start us, length us, event | category | flops | bytes accessed | tf_op | source)
XLA Modules:
  0.0 322.5 jit_solution(8568578363218023782)
XLA Ops:
  6.5 0.7 all-gather.5.cloned.1.call-update
  7.3 0.7 all-gather.7.cloned.1.call-update
  8.1 1.2 fusion.39
  9.3 55.6 %all-gather.5.cloned.1.call-done = bf16[1024,3072]{1,0:T(8,128)(2,1)} async-done(((bf16[64,3072]{1,0:T(8,128)(2,1)}), bf16[1024,3072]{1,0:T(8,128)(2,1)}) %all-gather.5.cloned.1.call-update) | async-done | bytes 6291472 | tf_op jit(solution)/shard_map/all_gather | solution.py:84
  64.9 4.8 %convolution_convert_fusion = bf16[256,3072]{1,0:T(8,128)(2,1)S(1)} fusion(bf16[1024,3072]{1,0:T(8,128)(2,1)} %all-gather.5.cloned.1.call-done, bf16[256,1024]{1,0:T(8,128)(2,1)} %param.12, f32[256]{0:T(256)S(1)} %add_rsqrt_fusion.1), kind=kOutput, calls=%fused_computation.40 | convolution fusion | flops 1612185600 | bytes 8389632 | tf_op jit(solution)/shard_map/dot_general | solution.py:73
  69.8 2.7 collective-permute-start
  72.5 2.6 collective-permute-start.1
  75.3 1.0 copy.15
  76.3 10.8 %collective-permute-done = bf16[256,2048]{1,0:T(8,128)(2,1)} collective-permute-done((bf16[256,2048]{1,0:T(8,128)(2,1)S(1)}, bf16[256,2048]{1,0:T(8,128)(2,1)}, u32[]{:S(2)}, u32[]{:S(2)}) %collective-permute-start) | collective-permute-done | bytes 1048608 | tf_op jit(solution)/shard_map/ppermute | solution.py:21
  87.1 6.1 %collective-permute-done.1 = bf16[256,2048]{1,0:T(8,128)(2,1)} collective-permute-done((bf16[256,2048]{1,0:T(8,128)(2,1)S(1)}, bf16[256,2048]{1,0:T(8,128)(2,1)}, u32[]{:S(2)}, u32[]{:S(2)}) %collective-permute-start.1) | collective-permute-done | bytes 1048608 | tf_op jit(solution)/shard_map/ppermute | solution.py:23
  93.2 1.7 pad_maximum_fusion
  94.9 0.3 fusion.78
  95.2 1.6 copy.16
  96.8 0.7 copy.17
  97.6 33.1 %while.26 = (s32[]{:T(128)}, bf16[16,256,64]{1,2,0:T(8,128)(2,1)S(1)}, bf16[16,256,64]{1,2,0:T(8,128)(2,1)}, bf16[16,768,64]{1,2,0:T(8,128)(2,1)}, bf16[16,768,6...) while((s32[]{:T(128)}, ...), condition=%wide.region_4.5_spmd.clone, body=%wide.region_1.4_spmd.clone.sunk | while | flops 52723200 | bytes 2633565 | solution.py:68
  97.6 1.4 fusion.111
  99.3 0.4 fusion.113
  99.7 1.4 fusion.111
  101.4 0.4 fusion.113
  101.8 1.4 fusion.111
  103.4 0.4 fusion.113
  103.8 1.4 fusion.111
  105.5 0.4 fusion.113
  105.9 1.4 fusion.111
  107.6 0.4 fusion.113
  108.0 1.4 fusion.111
  109.6 0.4 fusion.113
  110.0 1.4 fusion.111
  111.7 0.4 fusion.113
  112.1 1.4 fusion.111
  113.7 0.4 fusion.113
  114.1 1.4 fusion.111
  115.8 0.4 fusion.113
  116.2 1.4 fusion.111
  117.9 0.4 fusion.113
  118.3 1.4 fusion.111
  119.9 0.4 fusion.113
  120.3 1.4 fusion.111
  122.0 0.4 fusion.113
  122.4 1.4 fusion.111
  124.1 0.4 fusion.113
  124.5 1.4 fusion.111
  126.1 0.4 fusion.113
  126.5 1.4 fusion.111
  128.2 0.4 fusion.113
  128.6 1.4 fusion.111
  130.3 0.4 fusion.113
  130.7 2.4 bitcast_reduce_fusion
  133.1 16.1 %all_gather.21 = bf16[128,1024]{1,0:T(8,128)(2,1)S(1)} all-gather(bf16[8,1024]{1,0:T(8,128)(2,1)S(1)} %multiply_convert_fusion.2), channel_id=1, replica_groups=mesh['doc'=32,'seq'=16] {'seq'}, dimensions={0}, use_global_device_ids=true | all-gather | bytes 278528 | tf_op jit(solution)/shard_map/all_gather | solution.py:95
  149.7 0.4 fusion.80
  150.1 0.4 fusion.38
  150.6 0.9 convolution_convert_fusion.2
  151.6 0.5 all-gather.11.cloned.1.call-update
  152.4 2.3 convolution_convert_fusion.1
  154.9 112.5 %all-reduce.2.cloned.1.call-done = bf16[128,1024]{1,0:T(8,128)(2,1)} async-done(((bf16[128,1024]{1,0:T(8,128)(2,1)}), bf16[128,1024]{1,0:T(8,128)(2,1)}) %all-reduce.2.cloned.1.call-update) | async-done | bytes 262160 | tf_op jit(solution)/shard_map/psum | solution.py:108
  267.4 1.1 fusion.41
  268.6 1.2 convolution_convert_fusion.7
  269.8 1.2 convolution_convert_fusion.6
  271.1 16.9 %all_gather.22 = bf16[128,2048]{0,1:T(8,128)(2,1)S(1)} all-gather(bf16[128,128]{0,1:T(8,128)(2,1)S(1)} %pad_maximum_fusion.1), channel_id=1, replica_groups=mesh['doc'=32,'seq'=16] {'seq'}, dimensions={1}, use_global_device_ids=true | all-gather | bytes 557056 | tf_op jit(solution)/shard_map/all_gather | solution.py:118
  288.0 0.3 copy.29
  288.3 0.3 copy.30
  288.7 7.1 %while.25 = (s32[]{:T(128)}, bf16[16,256,64]{1,2,0:T(8,128)(2,1)S(1)}, bf16[16,256,64]{1,2,0:T(8,128)(2,1)S(1)}, bf16[16,128,64]{2,1,0:T(8,128)(2,1)S(1)}, bf16[16,128,64]{2,1,0:T(8,128)(2,1)S(1)}, /*index=5*/s32[]{:T(128)}) while((s32[]{:T(128)}, bf16[16,256,64]{1,2,0:T(8,128)(2,1)S(1)}, bf16[16,256,64]{1,2,0:T(8,128)(2,1)S(1)}, ...), condition=%wide.region_15.16_spmd, body=%wide.region_12.15_spmd.sunk | while | flops 8617474 | bytes 531525 | solution.py:68
  295.8 17.0 %all-gather.11.cloned.1.call-done = bf16[1024,1024]{1,0:T(8,128)(2,1)} async-done(((bf16[64,1024]{1,0:T(8,128)(2,1)}), bf16[1024,1024]{1,0:T(8,128)(2,1)}) %all-gather.11.cloned.1.call-update) | async-done | bytes 2097168 | tf_op jit(solution)/shard_map/all_gather | solution.py:127
  312.8 3.1 fusion.37
  (100 shorter events, 12.7 us)
Async XLA Ops:
  6.5 144.0 %copy-start = (bf16[64,1024]{1,0:T(8,128)(2,1)S(1)}, bf16[64,1024]{1,0:T(8,128)(2,1)}, u32[]{:S(2)}) copy-start(bf16[64,1024]{1,0:T(8,128)(2,1)} %param.16) | copy-start | bytes 393220
  6.5 58.4 %all-gather.5.cloned.1.call-start = ((), (), s32[]{:S(2)}) async-start(), calls=%async_computation | async-start | bytes 6684672 | tf_op jit(solution)/shard_map/all_gather | solution.py:84
  7.3 123.4 %all-gather.7.cloned.1.call-start = ((), (), s32[]{:S(2)}) async-start(), calls=%async_computation.1 | async-start | bytes 2228224 | tf_op jit(solution)/shard_map/all_gather | solution.py:90
  8.0 144.4 %all-gather.9.cloned.1.call-start = ((), (), s32[]{:S(2)}) async-start(), calls=%async_computation.2 | async-start | bytes 2228224 | tf_op jit(solution)/shard_map/all_gather | solution.py:124
  69.8 17.2 %collective-permute-start = (bf16[256,2048]{1,0:T(8,128)(2,1)S(1)}, bf16[256,2048]{1,0:T(8,128)(2,1)}, u32[]{:S(2)}, u32[]{:S(2)}) collective-permute-start(bf16[256,2048]{1,0:T(8,128)(2,1)S(1)} %slice.45), channel_id=1, source_target_pairs={{0,1},{1,2},{2,3},{3,4},{4,5},{5,6},{6,7},{7,8},{8,9},{9,10},{10,1... | collective-permute-start | bytes 3145736 | tf_op jit(solution)/shard_map/ppermute | solution.py:21
  72.5 20.7 %collective-permute-start.1 = (bf16[256,2048]{1,0:T(8,128)(2,1)S(1)}, bf16[256,2048]{1,0:T(8,128)(2,1)}, u32[]{:S(2)}, u32[]{:S(2)}) collective-permute-start(bf16[256,2048]{1,0:T(8,128)(2,1)S(1)} %slice.45), channel_id=1, source_target_pairs={{1,0},{2,1},{3,2},{4,3},{5,4},{6,5},{7,6},{8,7},{9,8},{10,9},{11,1... | collective-permute-start | bytes 3145736 | tf_op jit(solution)/shard_map/ppermute | solution.py:23
  75.2 192.3 %all-reduce.2.cloned.1.call-start = ((), (), s32[]{:S(2)}) async-start(), calls=%async_computation.3 | async-start | bytes 524288 | tf_op jit(solution)/shard_map/psum | solution.py:108
  97.6 33.1 %copy-start.1 = (bf16[256,1024]{1,0:T(8,128)(2,1)S(1)}, bf16[256,1024]{1,0:T(8,128)(2,1)}, u32[]{:S(2)}) copy-start(bf16[256,1024]{1,0:T(8,128)(2,1)} %param.12) | copy-start | bytes 1572868
  130.7 18.7 %copy-start.2 = (bf16[1024,3,64]{0,2,1:T(8,128)(2,1)S(1)}, bf16[1024,3,64]{0,2,1:T(8,128)(2,1)}, u32[]{:S(2)}) copy-start(bf16[1024,3,64]{0,2,1:T(8,128)(2,1)} %param.15) | copy-start | bytes 1179652
  151.5 161.3 %all-gather.11.cloned.1.call-start = ((), (), s32[]{:S(2)}) async-start(), calls=%async_computation.4 | async-start | bytes 2228224 | tf_op jit(solution)/shard_map/all_gather | solution.py:127
  152.3 116.3 %copy-start.3 = (bf16[1024,2,64]{0,2,1:T(8,128)(2,1)S(1)}, bf16[1024,2,64]{0,2,1:T(8,128)(2,1)}, u32[]{:S(2)}) copy-start(bf16[1024,2,64]{0,2,1:T(8,128)(2,1)} %param.18) | copy-start | bytes 786436
Sparse Core Ops, SparseCore 0:
  9.5 55.3 all-gather.4
  67.0 41.1 all-gather.6
  110.3 42.0 all-gather.8
  154.6 112.8 all-reduce.1
  269.6 43.1 all-gather.10
where the time goes:
time: 323 us; the launch traced here: 322 us
  waiting for transfers between devices  204 us (63%)
  matrix products  51.4 us (16%)
  blocking collectives  33 us (10%)
  between operations  13.4 us (4%)
  other arithmetic  9.66 us (3%)
  starting transfers between devices  5.46 us (2%)
  local copies, waits for them, and re-layouts  4.62 us (1%)
    psum x1, waiting for transfers between devices, local(): lax.psum(head_term.astype(jnp.bfloat16), 'seq').astype(jnp.float32)  113 us
    all_gather x1, waiting for transfers between devices, local(): lax.all_gather(bottom_qkv, 'seq', axis=0, tiled=True)  55.6 us
    dot_general x33, matrix products, one_head(): jnp.dot(query_h, key_h.T, preferred_element_type=jnp.float32) * score_scale  25.3 us
    all_gather x1, waiting for transfers between devices, local(): lax.all_gather(cross_out, 'seq', axis=0, tiled=True)  17 us
    all_gather x1, blocking collectives, local(): gathered = lax.all_gather(stacked, 'seq', axis=1, tiled=True)  16.9 us
    all_gather x1, blocking collectives, local(): all_units = lax.all_gather(pooled, 'seq', axis=0, tiled=True)  16.1 us
    dot_general x4, matrix products, fold_rows(): return jnp.dot(operand, shard_rows, preferred_element_type=jnp.float32)  12.7 us
    ppermute x1, waiting for transfers between devices, padded(): lax.ppermute(tail, axis, [(i, (i + 1) % count) for i in range(ends)])  10.8 us
  transfers between devices with their start and end apart: 7, of which 6 were waited for; matrix products, arithmetic and copies ran while one was open for 19% of the time, Pallas kernels for 0%

commit v1 on v0

--- a/solution.py
+++ b/solution.py
@@ -105,7 +105,9 @@
     )
     top_att = attend(top_q, top_k, top_v, None, local_heads)
     head_term = jnp.dot(top_att, top_out, preferred_element_type=jnp.float32)
-    head_total = lax.psum(head_term.astype(jnp.bfloat16), "seq").astype(jnp.float32)
+    head_total = jnp.sum(lax.all_gather(head_term.astype(jnp.bfloat16), "seq"), axis=0).astype(
+        jnp.float32
+    )
     top_units = (all_units.astype(jnp.float32) + head_total).astype(jnp.bfloat16)
     upper_norm = normed(top_units)
     part_keys = jnp.dot(upper_norm, cross_kv[:, 0, :], preferred_element_type=jnp.float32).astype(

time: 323 us -> 252 us (0.78)
  waiting for transfers between devices: 204 us -> 132 us
    psum x1 -> x0, waiting for transfers between devices: 113 us -> none  [local(): lax.psum(head_term.astype(jnp.bfloat16), 'seq').astype(jnp.float32)]
    all_gather x0 -> x1, waiting for transfers between devices: none -> 43.4 us  [local(): lax.all_gather(head_term.astype(jnp.bfloat16), 'seq')]
  transfers between devices with their start and end apart: 7 -> 7, of which waited for: 6 -> 5; matrix products, arithmetic and copies ran while one was open for 19% -> 25% of each run, Pallas kernels for 0% -> 0%
where the time goes in v1:
time: 252 us; the launch traced here: 251 us
  waiting for transfers between devices  132 us (52%)
  matrix products  49.5 us (20%)
  blocking collectives  33.3 us (13%)
  between operations  13.4 us (5%)
  other arithmetic  11.9 us (5%)
  starting transfers between devices  5.51 us (2%)
  local copies, waits for them, and re-layouts  4.65 us (2%)
    all_gather x1, waiting for transfers between devices, local(): lax.all_gather(bottom_qkv, 'seq', axis=0, tiled=True)  55.6 us
    all_gather x1, waiting for transfers between devices, local(): lax.all_gather(head_term.astype(jnp.bfloat16), 'seq')  43.4 us
    dot_general x33, matrix products, one_head(): jnp.dot(query_h, key_h.T, preferred_element_type=jnp.float32) * score_scale  25.3 us
    all_gather x1, blocking collectives, local(): gathered = lax.all_gather(stacked, 'seq', axis=1, tiled=True)  17.3 us
    all_gather x1, blocking collectives, local(): all_units = lax.all_gather(pooled, 'seq', axis=0, tiled=True)  16 us
    all_gather x1, waiting for transfers between devices, local(): lax.all_gather(cross_out, 'seq', axis=0, tiled=True)  14.1 us
    dot_general x4, matrix products, fold_rows(): return jnp.dot(operand, shard_rows, preferred_element_type=jnp.float32)  12.7 us
    ppermute x1, waiting for transfers between devices, padded(): lax.ppermute(tail, axis, [(i, (i + 1) % count) for i in range(ends)])  10.7 us
  transfers between devices with their start and end apart: 7, of which 5 were waited for; matrix products, arithmetic and copies ran while one was open for 25% of the time, Pallas kernels for 0%

profile of v1, /device:TPU:1, one launch (start us, length us, event | category | flops | bytes accessed | tf_op | source)
XLA Modules:
  0.0 251.0 jit_solution(5189037876436451069)
XLA Ops:
  6.5 0.7 all-gather.7.cloned.1.call-update
  7.3 0.7 all-gather.9.cloned.1.call-update
  8.1 1.2 fusion.39
  9.3 55.6 %all-gather.7.cloned.1.call-done = bf16[1024,3072]{1,0:T(8,128)(2,1)} async-done(((bf16[64,3072]{1,0:T(8,128)(2,1)}), bf16[1024,3072]{1,0:T(8,128)(2,1)}) %all-gather.7.cloned.1.call-update) | async-done | bytes 6291472 | tf_op jit(solution)/shard_map/all_gather | solution.py:84
  64.9 4.8 %convolution_convert_fusion = bf16[256,3072]{1,0:T(8,128)(2,1)S(1)} fusion(bf16[1024,3072]{1,0:T(8,128)(2,1)} %all-gather.7.cloned.1.call-done, bf16[256,1024]{1,0:T(8,128)(2,1)} %param.12, f32[256]{0:T(256)S(1)} %add_rsqrt_fusion.1), kind=kOutput, calls=%fused_computation.40 | convolution fusion | flops 1612185600 | bytes 8389632 | tf_op jit(solution)/shard_map/dot_general | solution.py:73
  69.8 2.7 %collective-permute-start = (bf16[256,2048]{1,0:T(8,128)(2,1)S(1)}, bf16[256,2048]{1,0:T(8,128)(2,1)}, u32[]{:S(2)}, u32[]{:S(2)}) collective-permute-start(bf16[256,2048]{1,0:T(8,128)(2,1)S(1)} %slice.45), channel_id=1, source_target_pairs={{0,1},{1,2},{2,3},{3,4},{4,5},{5,6},{6,7},{7,8},{8,9},{9,10},{10,1... | collective-permute-start | bytes 3145736 | tf_op jit(solution)/shard_map/ppermute | solution.py:21
  72.5 2.7 %collective-permute-start.1 = (bf16[256,2048]{1,0:T(8,128)(2,1)S(1)}, bf16[256,2048]{1,0:T(8,128)(2,1)}, u32[]{:S(2)}, u32[]{:S(2)}) collective-permute-start(bf16[256,2048]{1,0:T(8,128)(2,1)S(1)} %slice.45), channel_id=1, source_target_pairs={{1,0},{2,1},{3,2},{4,3},{5,4},{6,5},{7,6},{8,7},{9,8},{10,9},{11,1... | collective-permute-start | bytes 3145736 | tf_op jit(solution)/shard_map/ppermute | solution.py:23
  75.4 1.0 copy.25
  76.4 10.7 %collective-permute-done = bf16[256,2048]{1,0:T(8,128)(2,1)} collective-permute-done((bf16[256,2048]{1,0:T(8,128)(2,1)S(1)}, bf16[256,2048]{1,0:T(8,128)(2,1)}, u32[]{:S(2)}, u32[]{:S(2)}) %collective-permute-start) | collective-permute-done | bytes 1048608 | tf_op jit(solution)/shard_map/ppermute | solution.py:21
  87.1 6.1 %collective-permute-done.1 = bf16[256,2048]{1,0:T(8,128)(2,1)} collective-permute-done((bf16[256,2048]{1,0:T(8,128)(2,1)S(1)}, bf16[256,2048]{1,0:T(8,128)(2,1)}, u32[]{:S(2)}, u32[]{:S(2)}) %collective-permute-start.1) | collective-permute-done | bytes 1048608 | tf_op jit(solution)/shard_map/ppermute | solution.py:23
  93.2 1.7 pad_maximum_fusion
  94.9 0.3 fusion.78
  95.2 1.6 copy.26
  96.8 0.7 copy.27
  97.6 33.1 %while.26 = (s32[]{:T(128)}, bf16[16,256,64]{1,2,0:T(8,128)(2,1)S(1)}, bf16[16,256,64]{1,2,0:T(8,128)(2,1)}, bf16[16,768,64]{1,2,0:T(8,128)(2,1)}, bf16[16,768,6...) while((s32[]{:T(128)}, ...), condition=%wide.region_4.5_spmd.clone, body=%wide.region_1.4_spmd.clone.sunk | while | flops 52723200 | bytes 2633565 | solution.py:68
  97.6 1.4 fusion.111
  99.3 0.4 fusion.113
  99.7 1.4 fusion.111
  101.4 0.4 fusion.113
  101.8 1.4 fusion.111
  103.5 0.4 fusion.113
  103.9 1.4 fusion.111
  105.5 0.4 fusion.113
  105.9 1.4 fusion.111
  107.6 0.4 fusion.113
  108.0 1.4 fusion.111
  109.7 0.4 fusion.113
  110.1 1.4 fusion.111
  111.7 0.4 fusion.113
  112.1 1.4 fusion.111
  113.8 0.4 fusion.113
  114.2 1.4 fusion.111
  115.8 0.4 fusion.113
  116.2 1.4 fusion.111
  117.9 0.4 fusion.113
  118.3 1.4 fusion.111
  120.0 0.4 fusion.113
  120.4 1.4 fusion.111
  121.8 0.3 fusion.112
  122.0 0.4 fusion.113
  122.4 1.4 fusion.111
  124.1 0.4 fusion.113
  124.5 1.4 fusion.111
  126.2 0.4 fusion.113
  126.6 1.4 fusion.111
  128.2 0.4 fusion.113
  128.6 1.4 fusion.111
  130.3 0.4 fusion.113
  130.7 2.4 bitcast_reduce_fusion
  133.2 16.0 %all_gather.27 = bf16[128,1024]{1,0:T(8,128)(2,1)S(1)} all-gather(bf16[8,1024]{1,0:T(8,128)(2,1)S(1)} %multiply_convert_fusion.2), channel_id=1, replica_groups=mesh['doc'=32,'seq'=16] {'seq'}, dimensions={0}, use_global_device_ids=true | all-gather | bytes 278528 | tf_op jit(solution)/shard_map/all_gather | solution.py:95
  149.3 0.3 convolution_convert_fusion.6
  149.6 0.4 fusion.80
  150.1 0.4 fusion.38
  150.5 1.0 convolution_convert_fusion.2
  151.5 0.5 all-gather.13.cloned.1.call-update
  152.3 2.3 convolution_convert_fusion.1
  154.8 43.4 %all-gather.15.cloned.1.call-done = bf16[2048,1024]{1,0:T(8,128)(2,1)} async-done(((bf16[128,1024]{1,0:T(8,128)(2,1)}), bf16[2048,1024]{1,0:T(8,128)(2,1)}) %all-gather.15.cloned.1.call-update) | async-done | bytes 4194320 | tf_op jit(solution)/shard_map/all_gather | solution.py:108
  198.2 3.2 %reduce_sum.90 = bf16[128,1024]{1,0:T(8,128)(2,1)S(1)} reduce(bf16[16,128,1024]{2,1,0:T(8,128)(2,1)} %bitcast.110, bf16[]{:T(256)} %constant.77.clone.1), dimensions={0}, to_apply=%region_10.11 | reduce | flops 1966080 | bytes 4456450 | tf_op jit(solution)/shard_map/reduce_sum | solution.py:108
  202.1 17.3 %all_gather.30 = bf16[128,2048]{0,1:T(8,128)(2,1)S(1)} all-gather(bf16[128,128]{0,1:T(8,128)(2,1)S(1)} %pad_maximum_fusion.1), channel_id=1, replica_groups=mesh['doc'=32,'seq'=16] {'seq'}, dimensions={1}, use_global_device_ids=true | all-gather | bytes 557056 | tf_op jit(solution)/shard_map/all_gather | solution.py:120
  219.5 0.3 copy.39
  219.8 0.3 copy.40
  220.2 7.1 %while.25 = (s32[]{:T(128)}, bf16[16,256,64]{1,2,0:T(8,128)(2,1)S(1)}, bf16[16,256,64]{1,2,0:T(8,128)(2,1)S(1)}, bf16[16,128,64]{2,1,0:T(8,128)(2,1)S(1)}, bf16[16,128,64]{2,1,0:T(8,128)(2,1)S(1)}, /*index=5*/s32[]{:T(128)}) while((s32[]{:T(128)}, bf16[16,256,64]{1,2,0:T(8,128)(2,1)S(1)}, bf16[16,256,64]{1,2,0:T(8,128)(2,1)S(1)}, ...), condition=%wide.region_15.16_spmd, body=%wide.region_12.15_spmd.sunk | while | flops 8617474 | bytes 531525 | solution.py:68
  227.3 14.1 %all-gather.13.cloned.1.call-done = bf16[1024,1024]{1,0:T(8,128)(2,1)} async-done(((bf16[64,1024]{1,0:T(8,128)(2,1)}), bf16[1024,1024]{1,0:T(8,128)(2,1)}) %all-gather.13.cloned.1.call-update) | async-done | bytes 2097168 | tf_op jit(solution)/shard_map/all_gather | solution.py:129
  241.4 3.1 %fusion.37 = bf16[256,1024]{1,0:T(8,128)(2,1)} fusion(f32[256,1024]{1,0:T(8,128)S(1)} %get-tuple-element.163, bf16[256,1024]{0,1:T(8,128)(2,1)S(1)} %bitcast.113, bf16[1024,1024]{1,0:T(8,128)(2,1)} %all-gather.13.cloned.1.call-done), kind=kOutput, calls=%fused_computation.49 | convolution fusion | flops 537395200 | bytes 4194304 | tf_op jit(solution)/shard_map/dot_general | solution.py:73
  (101 shorter events, 12.7 us)
Async XLA Ops:
  6.5 144.0 %copy-start = (bf16[64,1024]{1,0:T(8,128)(2,1)S(1)}, bf16[64,1024]{1,0:T(8,128)(2,1)}, u32[]{:S(2)}) copy-start(bf16[64,1024]{1,0:T(8,128)(2,1)} %param.16) | copy-start | bytes 393220
  6.5 58.4 %all-gather.7.cloned.1.call-start = ((), (), s32[]{:S(2)}) async-start(), calls=%async_computation | async-start | bytes 6684672 | tf_op jit(solution)/shard_map/all_gather | solution.py:84
  7.3 123.5 %all-gather.9.cloned.1.call-start = ((), (), s32[]{:S(2)}) async-start(), calls=%async_computation.1 | async-start | bytes 2228224 | tf_op jit(solution)/shard_map/all_gather | solution.py:90
  8.0 144.3 %all-gather.11.cloned.1.call-start = ((), (), s32[]{:S(2)}) async-start(), calls=%async_computation.2 | async-start | bytes 2228224 | tf_op jit(solution)/shard_map/all_gather | solution.py:126
  69.8 17.2 %collective-permute-start = (bf16[256,2048]{1,0:T(8,128)(2,1)S(1)}, bf16[256,2048]{1,0:T(8,128)(2,1)}, u32[]{:S(2)}, u32[]{:S(2)}) collective-permute-start(bf16[256,2048]{1,0:T(8,128)(2,1)S(1)} %slice.45), channel_id=1, source_target_pairs={{0,1},{1,2},{2,3},{3,4},{4,5},{5,6},{6,7},{7,8},{8,9},{9,10},{10,1... | collective-permute-start | bytes 3145736 | tf_op jit(solution)/shard_map/ppermute | solution.py:21
  72.5 20.7 %collective-permute-start.1 = (bf16[256,2048]{1,0:T(8,128)(2,1)S(1)}, bf16[256,2048]{1,0:T(8,128)(2,1)}, u32[]{:S(2)}, u32[]{:S(2)}) collective-permute-start(bf16[256,2048]{1,0:T(8,128)(2,1)S(1)} %slice.45), channel_id=1, source_target_pairs={{1,0},{2,1},{3,2},{4,3},{5,4},{6,5},{7,6},{8,7},{9,8},{10,9},{11,1... | collective-permute-start | bytes 3145736 | tf_op jit(solution)/shard_map/ppermute | solution.py:23
  75.2 123.0 %all-gather.15.cloned.1.call-start = ((), (), s32[]{:S(2)}) async-start(), calls=%async_computation.4 | async-start | bytes 4456448 | tf_op jit(solution)/shard_map/all_gather | solution.py:108
  97.6 33.1 %copy-start.1 = (bf16[256,1024]{1,0:T(8,128)(2,1)S(1)}, bf16[256,1024]{1,0:T(8,128)(2,1)}, u32[]{:S(2)}) copy-start(bf16[256,1024]{1,0:T(8,128)(2,1)} %param.12) | copy-start | bytes 1572868
  130.7 18.6 %copy-start.2 = (bf16[1024,3,64]{0,2,1:T(8,128)(2,1)S(1)}, bf16[1024,3,64]{0,2,1:T(8,128)(2,1)}, u32[]{:S(2)}) copy-start(bf16[1024,3,64]{0,2,1:T(8,128)(2,1)} %param.15) | copy-start | bytes 1179652
  151.5 89.9 %all-gather.13.cloned.1.call-start = ((), (), s32[]{:S(2)}) async-start(), calls=%async_computation.3 | async-start | bytes 2228224 | tf_op jit(solution)/shard_map/all_gather | solution.py:129
  198.2 3.4 %copy-start.3 = (bf16[1024,2,64]{0,2,1:T(8,128)(2,1)S(1)}, bf16[1024,2,64]{0,2,1:T(8,128)(2,1)}, u32[]{:S(2)}) copy-start(bf16[1024,2,64]{0,2,1:T(8,128)(2,1)} %param.18) | copy-start | bytes 786436
Sparse Core Ops, SparseCore 0:
  9.5 55.3 all-gather.6
  67.0 41.6 all-gather.8
  110.8 41.3 all-gather.10
  154.2 43.9 all-gather.14
  200.2 41.1 all-gather.12
